TPU v7x, 32 devices: a whole 2x2x4 slice. The times are simulated.
32 devices in a mesh: users: 2 (over x), hist: 8 (over z, y), head: 2 (over core).
Axes of the slice: x: 2, y: 2, z: 4, core: 2. Of those that a mesh axis runs over, the one named last changes fastest.
Arguments:
- candidates: bfloat16 [2048, 512], P(('users', 'hist')), parts along dimension 0, may hold values from -6 to 6
- key_cache: bfloat16 [2, 32768, 512], P(None, ('users', 'hist'), 'head'), parts along dimension 1, may hold values from -6 to 6
- value_cache: bfloat16 [2, 32768, 512], P(None, ('users', 'hist'), 'head'), parts along dimension 1, may hold values from -6 to 6
- w_in: bfloat16 [2, 512, 4, 512], P(None, None, None, 'head'), may hold values from -0.25 to 0.25
- w_out: bfloat16 [2, 512, 512], P(None, 'head'), may hold values from -0.25 to 0.25
- rab_table: float32 [2, 32, 8], P(None, None, 'head'), may hold values from -4 to 4
- hist_len: int32 [16], P(('users', 'hist')), parts along dimension 0, may hold values from 1 to 2048, 8192 in all
- hist_bucket: int32 [32768], P(('users', 'hist')), parts along dimension 0, may hold values from 0 to 31
- visible: int32 [8, 128], P(None, ('users', 'hist')), parts along dimension 1, may hold values 0 or 1
Outputs:
- candidate_out: bfloat16 [2048, 512], P(('users', 'hist')), parts along dimension 0
There are 2 independent parts, one for each index of `users`. A program takes and returns all parts, laid end to end along the dimension named above; an argument that names none is the same for every part. Nothing has to cross between parts.
Inputs may be any that keep to these rules, and one draw needn't show every extreme that they name: `hist_len`: entry s counts the valid events at the start of history shard s; the entries sum to 8192 and the largest is 2048. visible[m, b] is 1 where microbatch m sees history events b * 256 to (b + 1) * 256 - 1.
All inputs are finite; a program needn't handle non-finite values.
Results may differ from a plain program's by a relative error of at most 0.019.
Values may be sent and summed in bfloat16 or wider, within the bound.
No kernel may reach another device: no remote copies, remote signals or barrier semaphores. Data moves between devices by JAX's collectives and lax.ppermute only.
A program may use at most 64 MiB of HBM per device.

v0:
```python
import jax
import jax.numpy as jnp
from jax import lax
from jax.sharding import PartitionSpec as P

D = 512
HEADS = 8
DH = 64
LAYERS = 2
NB = 32
BLOCK = 256
MICRO = 8
C = 1024
epsilon = 1e-05


def shards(
    candidates, key_cache, value_cache, w_in, w_out, rab_table, hist_len, hist_bucket, visible
):
    width = HEADS * DH
    factor = DH ** (-0.5)
    local_len = hist_len[0]
    hist_dev = key_cache.shape[1]
    width_local = key_cache.shape[2]
    heads_local = width_local // DH
    key_block = min(512, hist_dev)
    row_count = candidates.shape[0]
    visible_float = visible.astype(jnp.float32)
    stream = lax.all_gather(candidates, "hist", axis=0, tiled=True).astype(jnp.float32)
    for layer_index in range(LAYERS):
        project_average = jnp.mean(stream, axis=-1, keepdims=True)
        centred = stream - project_average
        variance = jnp.mean(centred * centred, axis=-1, keepdims=True)
        normed = (centred * lax.rsqrt(variance + epsilon)).astype(jnp.bfloat16)
        projected = jnp.dot(
            normed,
            w_in[layer_index].reshape(D, 4 * width_local),
            preferred_element_type=jnp.float32,
        )
        projected = jax.nn.silu(projected).astype(jnp.bfloat16).reshape(-1, 4, width_local)
        queries = projected[:, 0]
        keys_new = projected[:, 1]
        values_new = projected[:, 2]
        gates = projected[:, 3]
        one_hot = (hist_bucket[:, None] == jnp.arange(NB, dtype=jnp.int32)[None, :]).astype(
            jnp.float32
        )
        bias = jnp.dot(one_hot, rab_table[layer_index], precision=lax.Precision.HIGHEST)
        attend_query_count = queries.shape[0]
        micro_ids = jnp.arange(attend_query_count, dtype=jnp.int32) // (C // MICRO)
        picking = (micro_ids[:, None] == jnp.arange(MICRO, dtype=jnp.int32)[None, :]).astype(
            jnp.float32
        )
        visible_rows = jnp.dot(picking, visible_float, precision=lax.Precision.HIGHEST)
        attend_query_heads = queries.reshape(attend_query_count, heads_local, DH)
        cached_keys = key_cache[layer_index]
        cached_values = value_cache[layer_index]

        def block_step(block_index, summed):
            key_start = block_index * key_block

            def compute(held):
                key_part = lax.dynamic_slice_in_dim(cached_keys, key_start, key_block, 0).reshape(
                    key_block, heads_local, DH
                )
                value_part = lax.dynamic_slice_in_dim(
                    cached_values, key_start, key_block, 0
                ).reshape(key_block, heads_local, DH)
                bias_part = lax.dynamic_slice_in_dim(bias, key_start, key_block, 0)
                visible_part = lax.dynamic_slice_in_dim(
                    visible_rows, key_start // BLOCK, key_block // BLOCK, 1
                )
                positions = key_start + jnp.arange(key_block, dtype=jnp.int32)
                valid = (positions < local_len).astype(jnp.float32)
                masking = (
                    jnp.repeat(visible_part, BLOCK, axis=1, total_repeat_length=key_block)
                    * valid[None, :]
                )
                scores = jnp.einsum(
                    "rhd,khd->hrk", attend_query_heads, key_part, preferred_element_type=jnp.float32
                )
                scores = scores * factor + bias_part.T[:, None, :]
                weights = (jax.nn.silu(scores) * masking[None]).astype(jnp.bfloat16)
                return held + jnp.einsum(
                    "hrk,khd->rhd", weights, value_part, preferred_element_type=jnp.float32
                )

            return lax.cond(key_start < local_len, compute, lambda held: held, summed)

        summed = lax.fori_loop(
            0,
            hist_dev // key_block,
            block_step,
            jnp.zeros((attend_query_count, heads_local, DH), jnp.float32),
        )
        terms = summed.reshape(attend_query_count, width_local)
        attended = lax.psum(terms.astype(jnp.bfloat16), "hist").astype(jnp.float32)
        finish_attended = attended
        query_count = finish_attended.shape[0]
        query_heads = queries.astype(jnp.float32).reshape(query_count, heads_local, DH)
        key_heads = keys_new.astype(jnp.float32).reshape(query_count, heads_local, DH)
        value_heads = values_new.astype(jnp.float32).reshape(query_count, heads_local, DH)
        own_score = jax.nn.silu(jnp.sum(query_heads * key_heads, axis=-1) * factor)
        finish_attended = finish_attended + (own_score[..., None] * value_heads).reshape(
            query_count, width_local
        )
        totals = lax.psum(
            (
                jnp.sum(finish_attended, axis=-1),
                jnp.sum(finish_attended * finish_attended, axis=-1),
            ),
            "head",
        )
        average = (totals[0] / width)[:, None]
        squares = (totals[1] / width)[:, None]
        normalized = (finish_attended - average) * lax.rsqrt(squares - average * average + epsilon)
        gated = (normalized * gates.astype(jnp.float32)).astype(jnp.bfloat16)
        update = lax.psum(
            jnp.dot(gated, w_out[layer_index], preferred_element_type=jnp.float32).astype(
                jnp.bfloat16
            ),
            "head",
        ).astype(jnp.float32)
        stream = stream + update
    own_start = lax.axis_index("hist") * row_count
    return lax.dynamic_slice_in_dim(stream, own_start, row_count, 0).astype(jnp.bfloat16)


def solution(mesh):
    placed = (
        P(("users", "hist"), None),
        P(None, ("users", "hist"), "head"),
        P(None, ("users", "hist"), "head"),
        P(None, None, None, "head"),
        P(None, "head", None),
        P(None, None, "head"),
        P(("users", "hist")),
        P(("users", "hist")),
        P(None, ("users", "hist")),
    )
    return jax.shard_map(
        shards, mesh=mesh, in_specs=placed, out_specs=P(("users", "hist"), None), check_vma=False
    )
```

profile of v0, /device:TPU:0, one launch (start us, length us, event | category | flops | bytes accessed | tf_op | source)
XLA Modules:
  0.0 378.6 jit_solution(7019134319419471442)
XLA Ops:
  7.3 3.3 fusion.74
  13.6 1.5 copy.18
  16.8 1.5 copy.19
  19.4 33.2 %all-gather.2.cloned.1.call-done = bf16[1024,512]{1,0:T(8,128)(2,1)} async-done(((bf16[128,512]{1,0:T(8,128)(2,1)}), bf16[1024,512]{1,0:T(8,128)(2,1)}) %all-gather.2.cloned.1.call-update) | async-done | bytes 1048592 | tf_op jit(solution)/shard_map/all_gather | solution.py:29
  52.6 1.5 convert_reduce_fusion
  54.1 1.7 fusion.38
  55.9 2.6 multiply_convert_fusion.1
  62.0 15.1 %while.34 = (s32[]{:T(128)}, f32[1024,4,64]{0,2,1:T(8,128)}, s32[]{:T(128)}, bf16[2048,256]{0,1:T(8,128)(2,1)}, bf16[2048,256]{0,1:T(8,128)(2,1)}, /*index=5*/bf...) while((s32[]{:T(128)}, f32[1024,4,64]{0,2,1:T(8,128)}, ...), condition=%wide.region_5.7_spmd, body=%wide.region_2.6_spmd.sunk | while | flops 554437120 | bytes 14733740 | solution.py:90
  62.6 12.4 %conditional.4 = (f32[1024,4,64]{0,2,1:T(8,128)}) conditional(s32[]{:T(128)} %convert_element_type.273, f32[1024,4,64]{0,2,1:T(8,128)} %get-tuple-element.543, (s32[]{:T(128)}, bf16[2048,256]{0,1:T(8,128)(2,1)}, bf16[2048,256]{0,1:T(8,128)(2,1)}, bf16[1024,4,64]{0,2,1:T(8,128)(2,1)}, f32[2048,4]{0,1:T(4,128)S(1)}, /*index=5*/f32[1024,8]{0,1:T(8,128)S(1)}, ...), branch_computations={%region_3.3_spmd, %region_4.5_spmd} | conditional | flops 554437120 | bytes 14733549 | solution.py:88
  63.4 1.8 gather_fusion
  65.9 1.5 bitcast_multiply_fusion.1
  68.5 6.6 %fusion.12 = f32[1024,4,64]{0,2,1:T(8,128)} fusion(f32[1024,4,64]{0,2,1:T(8,128)} %get-tuple-element.336, bf16[512,4,64]{0,2,1:T(8,128)(2,1)S(1)} %bitcast.148, f32[1024,512]{0,1:T(8,128)} %bitcast_multiply_fusion.1, f32[4,512]{1,0:T(4,128)S(1)} %dynamic-slice_bitcast_fusion, bf16[512,4,64]{0,2,1:T(8,128)(2,1)S(1)} %bitcast.147, ...), kind=kOutput, calls=%fused_computation.13 | convolution fusion | flops 553910272 | bytes 5251072 | tf_op jit(solution)/shard_map/while/body/eval_jaxpr/cond/branch_1_fun/hrk,khd->rhd/dot_general | solution.py:84
  77.1 2.2 convert_element_type.165
  79.6 108.4 %all-reduce.7.cloned.1.call-done = bf16[1024,256]{0,1:T(8,128)(2,1)} async-done(((bf16[1024,256]{0,1:T(8,128)(2,1)}), bf16[1024,256]{0,1:T(8,128)(2,1)}) %all-reduce.7.cloned.1.call-update) | async-done | bytes 524304 | tf_op jit(solution)/shard_map/psum | solution.py:97
  188.0 1.5 fusion.53
  189.5 2.5 all-reduce.1
  192.0 1.8 fusion.44
  193.8 2.5 convolution_convert_fusion.1
  199.2 1.5 copy.21
  201.4 13.7 %all-reduce.9.cloned.1.call-done = bf16[1024,512]{1,0:T(8,128)(2,1)} async-done(((bf16[1024,512]{1,0:T(8,128)(2,1)}), bf16[1024,512]{1,0:T(8,128)(2,1)}) %all-reduce.9.cloned.1.call-update) | async-done | bytes 1048592 | tf_op jit(solution)/shard_map/psum | solution.py:118
  215.1 1.7 fusion.72
  216.8 1.8 multiply_reduce_fusion
  218.6 2.6 multiply_convert_fusion
  223.1 14.0 %while.35 = (s32[]{:T(128)}, f32[1024,4,64]{0,2,1:T(8,128)S(1)}, s32[]{:T(128)}, bf16[2048,256]{0,1:T(8,128)(2,1)}, bf16[2048,256]{0,1:T(8,128)(2,1)}, /*index=5...) while((s32[]{:T(128)}, f32[1024,4,64]{0,2,1:T(8,128)S(1)}, ...), condition=%wide.region_18.20_spmd, body=%wide.region_15.19_spmd.sunk | while | flops 554437120 | bytes 14733740 | solution.py:90
  223.8 11.3 %conditional.5 = (f32[1024,4,64]{0,2,1:T(8,128)S(1)}) conditional(s32[]{:T(128)} %convert_element_type.274, f32[1024,4,64]{0,2,1:T(8,128)S(1)} %get-tuple-element.573, (s32[]{:T(128)}, bf16[2048,256]{0,1:T(8,128)(2,1)}, bf16[2048,256]{0,1:T(8,128)(2,1)}, bf16[1024,4,64]{0,2,1:T(8,128)(2,1)}, f32[2048,4]{0,1:T(4,128)S(1)}, ...), branch_computations={%region_16.17_spmd, %region_17.18_spmd} | conditional | flops 554437120 | bytes 14733549 | solution.py:88
  224.5 1.8 gather_fusion.1
  227.0 1.5 bitcast_multiply_fusion.3
  229.6 5.4 %fusion.30 = f32[1024,4,64]{0,2,1:T(8,128)S(1)} fusion(f32[1024,4,64]{0,2,1:T(8,128)S(1)} %get-tuple-element.353, bf16[512,4,64]{0,2,1:T(8,128)(2,1)S(1)} %bitcast.150, f32[1024,512]{0,1:T(8,128)} %bitcast_multiply_fusion.3, f32[4,512]{1,0:T(4,128)S(1)} %dynamic-slice_bitcast_fusion.1, bf16[512,4,64]{0,2,1:T(8,128)(2,1)S(1)} %bitcast.149, ...), kind=kOutput, calls=%fused_computation.34 | convolution fusion | flops 553910272 | bytes 5251072 | tf_op jit(solution)/shard_map/while/body/eval_jaxpr/cond/branch_1_fun/hrk,khd->rhd/dot_general | solution.py:84
  239.6 105.4 %all-reduce.11.cloned.1.call-done = bf16[1024,256]{0,1:T(8,128)(2,1)} async-done(((bf16[1024,256]{0,1:T(8,128)(2,1)}), bf16[1024,256]{0,1:T(8,128)(2,1)}) %all-reduce.11.cloned.1.call-update) | async-done | bytes 524304 | tf_op jit(solution)/shard_map/psum | solution.py:97
  346.3 2.5 all-reduce
  351.6 18.7 %all-reduce.13.cloned.1.call-done = bf16[1024,512]{1,0:T(8,128)(2,1)} async-done(((bf16[1024,512]{1,0:T(8,128)(2,1)}), bf16[1024,512]{1,0:T(8,128)(2,1)}) %all-reduce.13.cloned.1.call-update) | async-done | bytes 1048592 | tf_op jit(solution)/shard_map/psum | solution.py:118
  370.4 1.7 fusion.58
  (89 shorter events, 27.4 us)
Async XLA Ops:
  6.5 46.1 %all-gather.2.cloned.1.call-start = ((), (), s32[]{:S(2)}) async-start(), calls=%async_computation | async-start | bytes 1179648 | tf_op jit(solution)/shard_map/all_gather | solution.py:29
  7.3 180.8 %all-reduce.7.cloned.1.call-start = ((), (), s32[]{:S(2)}) async-start(), calls=%async_computation.1 | async-start | bytes 1048576 | tf_op jit(solution)/shard_map/psum | solution.py:97
  10.6 2.0 copy-start.8
  13.6 2.0 copy-start.9
  16.7 1.5 copy-start.16
  16.8 1.9 copy-start.15
  16.8 2.0 copy-start.17
  16.8 39.1 %copy-start.12 = (bf16[64,8,4,256]{3,1,2,0:T(8,128)(2,1)S(1)}, bf16[64,8,4,256]{3,1,2,0:T(8,128)(2,1)}, u32[]{:S(2)}) copy-start(bf16[64,8,4,256]{3,1,2,0:T(8,128)(2,1)} %copy.22) | copy-start | bytes 3145732
  52.6 3.3 copy-start
  58.5 1.3 copy-start.7
  77.1 2.3 copy-start.10
  77.1 2.3 copy-start.11
  79.3 135.8 %all-reduce.9.cloned.1.call-start = ((), (), s32[]{:S(2)}) async-start(), calls=%async_computation.2 | async-start | bytes 2097152 | tf_op jit(solution)/shard_map/psum | solution.py:118
  192.0 4.6 %copy-start.1 = (bf16[1,512,4,256]{3,2,1,0:T(4,128)(2,1)S(1)}, bf16[1,512,4,256]{3,2,1,0:T(4,128)(2,1)}, u32[]{:S(2)}) copy-start(bf16[1,512,4,256]{3,2,1,0:T(4,128)(2,1)} %get-tuple-element.422) | copy-start | bytes 3145732
  193.8 4.0 %copy-start.2 = (bf16[1,2048,256]{2,1,0:T(8,128)(2,1)S(1)}, bf16[1,2048,256]{2,1,0:T(8,128)(2,1)}, u32[]{:S(2)}) copy-start(bf16[1,2048,256]{2,1,0:T(8,128)(2,1)} %get-tuple-element.426) | copy-start | bytes 3145732
  196.3 148.6 %all-reduce.11.cloned.1.call-start = ((), (), s32[]{:S(2)}) async-start(), calls=%async_computation.3 | async-start | bytes 1048576 | tf_op jit(solution)/shard_map/psum | solution.py:97
  197.8 1.4 copy-start.3
  215.1 1.7 copy-start.4
  216.8 1.9 copy-start.13
  221.3 1.7 copy-start.5
  237.1 107.8 %copy-start.6 = (bf16[1024,1024]{0,1:T(8,128)(2,1)S(1)}, bf16[1024,1024]{0,1:T(8,128)(2,1)}, u32[]{:S(2)}) copy-start(bf16[1024,1024]{0,1:T(8,128)(2,1)} %copy-done.5) | copy-start | bytes 6291460
  238.0 132.3 %all-reduce.13.cloned.1.call-start = ((), (), s32[]{:S(2)}) async-start(), calls=%async_computation.4 | async-start | bytes 2097152 | tf_op jit(solution)/shard_map/psum | solution.py:118
  238.1 112.0 %copy-start.14 = (bf16[2,256,512]{2,1,0:T(8,128)(2,1)S(1)}, bf16[2,256,512]{2,1,0:T(8,128)(2,1)}, u32[]{:S(2)}) copy-start(bf16[2,256,512]{2,1,0:T(8,128)(2,1)} %param.27) | copy-start | bytes 1572868
Sparse Core Ops, SparseCore 0:
  9.5 43.0 all-gather.1
  79.4 108.5 all-reduce.6
  196.5 18.5 all-reduce.8
  238.2 106.7 all-reduce.10
  351.7 18.5 all-reduce.12
where the time goes:
time: 380 us; the launch traced here: 379 us
  waiting for transfers between devices  280 us (74%)
  local copies, waits for them, and re-layouts  26.2 us (7%)
  other arithmetic  24.7 us (6%)
  matrix products  23.1 us (6%)
  between operations  13.4 us (4%)
  loops' own time  5.58 us (1%)
  blocking collectives  4.99 us (1%)
    psum x2, waiting for transfers between devices, shards(): attended = lax.psum(terms.astype(jnp.bfloat16), 'hist').astype(jnp.float32)  214 us
    all_gather x1, waiting for transfers between devices, shards(): lax.all_gather(candidates, 'hist', axis=0, tiled=True).astype(jnp.float32)  33.2 us
    psum x2, waiting for transfers between devices, shards(): lax.psum(jnp.dot(gated, w_out[layer_index], preferred_element_type=jnp.fl...  32.4 us
    dot_general x2, matrix products, compute(): jnp.einsum('hrk,khd->rhd', weights, value_part, preferred_element_type=jn...  12 us
    unnamed x42, local copies, waits for them, and re-layouts  11.4 us
  transfers between devices with their start and end apart: 5, of which 5 were waited for; matrix products, arithmetic and copies ran while one was open for 5% of the time, Pallas kernels for 0%

commit v1 on v0

--- a/solution.py
+++ b/solution.py
@@ -115,11 +115,14 @@
         squares = (totals[1] / width)[:, None]
         normalized = (finish_attended - average) * lax.rsqrt(squares - average * average + epsilon)
         gated = (normalized * gates.astype(jnp.float32)).astype(jnp.bfloat16)
-        update = lax.psum(
-            jnp.dot(gated, w_out[layer_index], preferred_element_type=jnp.float32).astype(
-                jnp.bfloat16
+        update = jnp.sum(
+            lax.all_gather(
+                jnp.dot(gated, w_out[layer_index], preferred_element_type=jnp.float32).astype(
+                    jnp.bfloat16
+                ),
+                "head",
             ),
-            "head",
+            axis=0,
         ).astype(jnp.float32)
         stream = stream + update
     own_start = lax.axis_index("hist") * row_count

time: 380 us -> 366 us (0.963)
  waiting for transfers between devices: 280 us -> 262 us
  other arithmetic: 24.7 us -> 28.6 us
    psum x2 -> x0, waiting for transfers between devices: 32.4 us -> none  [shards(): lax.psum(jnp.dot(gated, w_out[layer_index], preferred_element_type=jnp.fl...]
    all_gather x0 -> x2, waiting for transfers between devices: none -> 14.8 us  [shards(): lax.all_gather(jnp.dot(gated, w_out[layer_index], preferred_element_type=...]
    reduce_sum x0 -> x2, other arithmetic: none -> 5.23 us  [shards(): jnp.sum(lax.all_gather(jnp.dot(gated, w_out[layer_index], preferred_eleme...]
    unnamed x42 -> x40, local copies, waits for them, and re-layouts: 11.4 us -> 11.4 us
where the time goes in v1:
time: 366 us; the launch traced here: 365 us
  waiting for transfers between devices  262 us (72%)
  other arithmetic  28.6 us (8%)
  local copies, waits for them, and re-layouts  26.2 us (7%)
  matrix products  23.1 us (6%)
  between operations  13.4 us (4%)
  loops' own time  5.58 us (2%)
  blocking collectives  4.99 us (1%)
    psum x2, waiting for transfers between devices, shards(): attended = lax.psum(terms.astype(jnp.bfloat16), 'hist').astype(jnp.float32)  214 us
    all_gather x1, waiting for transfers between devices, shards(): lax.all_gather(candidates, 'hist', axis=0, tiled=True).astype(jnp.float32)  33 us
    all_gather x2, waiting for transfers between devices, shards(): lax.all_gather(jnp.dot(gated, w_out[layer_index], preferred_element_type=...  14.8 us
    dot_general x2, matrix products, compute(): jnp.einsum('hrk,khd->rhd', weights, value_part, preferred_element_type=jn...  12 us
    unnamed x40, local copies, waits for them, and re-layouts  11.4 us
  transfers between devices with their start and end apart: 5, of which 5 were waited for; matrix products, arithmetic and copies ran while one was open for 5% of the time, Pallas kernels for 0%

profile of v1, /device:TPU:0, one launch (start us, length us, event | category | flops | bytes accessed | tf_op | source)
XLA Modules:
  0.0 364.6 jit_solution(7991527446865642305)
XLA Ops:
  7.3 3.3 fusion.74
  16.8 1.5 copy.19
  19.4 33.0 %all-gather.6.cloned.1.call-done = bf16[1024,512]{1,0:T(8,128)(2,1)} async-done(((bf16[128,512]{1,0:T(8,128)(2,1)}), bf16[1024,512]{1,0:T(8,128)(2,1)}) %all-gather.6.cloned.1.call-update) | async-done | bytes 1048592 | tf_op jit(solution)/shard_map/all_gather | solution.py:29
  52.5 1.5 convert_reduce_fusion
  54.0 1.7 fusion.38
  55.8 2.6 multiply_convert_fusion.1
  61.9 15.1 %while.34 = (s32[]{:T(128)}, f32[1024,4,64]{0,2,1:T(8,128)}, s32[]{:T(128)}, bf16[2048,256]{0,1:T(8,128)(2,1)}, bf16[2048,256]{0,1:T(8,128)(2,1)}, /*index=5*/bf...) while((s32[]{:T(128)}, f32[1024,4,64]{0,2,1:T(8,128)}, ...), condition=%wide.region_5.7_spmd, body=%wide.region_2.6_spmd.sunk | while | flops 554437120 | bytes 14733740 | solution.py:90
  62.5 12.4 %conditional.4 = (f32[1024,4,64]{0,2,1:T(8,128)}) conditional(s32[]{:T(128)} %convert_element_type.277, f32[1024,4,64]{0,2,1:T(8,128)} %get-tuple-element.543, (s32[]{:T(128)}, bf16[2048,256]{0,1:T(8,128)(2,1)}, bf16[2048,256]{0,1:T(8,128)(2,1)}, bf16[1024,4,64]{0,2,1:T(8,128)(2,1)}, f32[2048,4]{0,1:T(4,128)S(1)}, /*index=5*/f32[1024,8]{0,1:T(8,128)S(1)}, ...), branch_computations={%region_3.3_spmd, %region_4.5_spmd} | conditional | flops 554437120 | bytes 14733549 | solution.py:88
  63.3 1.8 gather_fusion
  65.8 1.5 bitcast_multiply_fusion.1
  68.4 6.6 %fusion.12 = f32[1024,4,64]{0,2,1:T(8,128)} fusion(f32[1024,4,64]{0,2,1:T(8,128)} %get-tuple-element.336, bf16[512,4,64]{0,2,1:T(8,128)(2,1)S(1)} %bitcast.150, f32[1024,512]{0,1:T(8,128)} %bitcast_multiply_fusion.1, f32[4,512]{1,0:T(4,128)S(1)} %dynamic-slice_bitcast_fusion, bf16[512,4,64]{0,2,1:T(8,128)(2,1)S(1)} %bitcast.149, ...), kind=kOutput, calls=%fused_computation.13 | convolution fusion | flops 553910272 | bytes 5251072 | tf_op jit(solution)/shard_map/while/body/eval_jaxpr/cond/branch_1_fun/hrk,khd->rhd/dot_general | solution.py:84
  77.0 2.2 convert_element_type.169
  79.5 108.4 %all-reduce.5.cloned.1.call-done = bf16[1024,256]{0,1:T(8,128)(2,1)} async-done(((bf16[1024,256]{0,1:T(8,128)(2,1)}), bf16[1024,256]{0,1:T(8,128)(2,1)}) %all-reduce.5.cloned.1.call-update) | async-done | bytes 524304 | tf_op jit(solution)/shard_map/psum | solution.py:97
  187.9 1.5 fusion.53
  189.3 2.5 all-reduce.1
  191.9 1.8 fusion.44
  193.6 2.5 convolution_convert_fusion.1
  201.2 4.9 %all-gather.8.cloned.1.call-done = bf16[2048,512]{1,0:T(8,128)(2,1)} async-done(((bf16[1024,512]{1,0:T(8,128)(2,1)}), bf16[2048,512]{1,0:T(8,128)(2,1)}) %all-gather.8.cloned.1.call-update) | async-done | bytes 2097168 | tf_op jit(solution)/shard_map/all_gather | solution.py:119
  206.1 2.6 reduce_sum.119
  209.0 1.8 multiply_reduce_fusion
  210.8 2.6 multiply_convert_fusion
  215.3 14.0 %while.35 = (s32[]{:T(128)}, f32[1024,4,64]{0,2,1:T(8,128)S(1)}, s32[]{:T(128)}, bf16[2048,256]{0,1:T(8,128)(2,1)}, bf16[2048,256]{0,1:T(8,128)(2,1)}, /*index=5...) while((s32[]{:T(128)}, f32[1024,4,64]{0,2,1:T(8,128)S(1)}, ...), condition=%wide.region_18.20_spmd, body=%wide.region_15.19_spmd.sunk | while | flops 554437120 | bytes 14733740 | solution.py:90
  216.0 11.3 %conditional.5 = (f32[1024,4,64]{0,2,1:T(8,128)S(1)}) conditional(s32[]{:T(128)} %convert_element_type.278, f32[1024,4,64]{0,2,1:T(8,128)S(1)} %get-tuple-element.573, (s32[]{:T(128)}, bf16[2048,256]{0,1:T(8,128)(2,1)}, bf16[2048,256]{0,1:T(8,128)(2,1)}, bf16[1024,4,64]{0,2,1:T(8,128)(2,1)}, f32[2048,4]{0,1:T(4,128)S(1)}, ...), branch_computations={%region_16.17_spmd, %region_17.18_spmd} | conditional | flops 554437120 | bytes 14733549 | solution.py:88
  216.8 1.8 gather_fusion.1
  219.3 1.5 bitcast_multiply_fusion.3
  221.9 5.4 %fusion.30 = f32[1024,4,64]{0,2,1:T(8,128)S(1)} fusion(f32[1024,4,64]{0,2,1:T(8,128)S(1)} %get-tuple-element.353, bf16[512,4,64]{0,2,1:T(8,128)(2,1)S(1)} %bitcast.152, f32[1024,512]{0,1:T(8,128)} %bitcast_multiply_fusion.3, f32[4,512]{1,0:T(4,128)S(1)} %dynamic-slice_bitcast_fusion.1, bf16[512,4,64]{0,2,1:T(8,128)(2,1)S(1)} %bitcast.151, ...), kind=kOutput, calls=%fused_computation.34 | convolution fusion | flops 553910272 | bytes 5251072 | tf_op jit(solution)/shard_map/while/body/eval_jaxpr/cond/branch_1_fun/hrk,khd->rhd/dot_general | solution.py:84
  231.8 105.4 %all-reduce.7.cloned.1.call-done = bf16[1024,256]{0,1:T(8,128)(2,1)} async-done(((bf16[1024,256]{0,1:T(8,128)(2,1)}), bf16[1024,256]{0,1:T(8,128)(2,1)}) %all-reduce.7.cloned.1.call-update) | async-done | bytes 524304 | tf_op jit(solution)/shard_map/psum | solution.py:97
  338.5 2.5 all-reduce
  342.4 1.5 convolution_convert_fusion
  343.9 9.9 %all-gather.10.cloned.1.call-done = bf16[2048,512]{1,0:T(8,128)(2,1)} async-done(((bf16[1024,512]{1,0:T(8,128)(2,1)}), bf16[2048,512]{1,0:T(8,128)(2,1)}) %all-gather.10.cloned.1.call-update) | async-done | bytes 2097168 | tf_op jit(solution)/shard_map/all_gather | solution.py:119
  353.8 2.6 reduce_sum.125
  356.4 1.6 fusion.58
  (89 shorter events, 29.2 us)
Async XLA Ops:
  6.5 46.0 %all-gather.6.cloned.1.call-start = ((), (), s32[]{:S(2)}) async-start(), calls=%async_computation | async-start | bytes 1179648 | tf_op jit(solution)/shard_map/all_gather | solution.py:29
  7.3 180.6 %all-reduce.5.cloned.1.call-start = ((), (), s32[]{:S(2)}) async-start(), calls=%async_computation.1 | async-start | bytes 1048576 | tf_op jit(solution)/shard_map/psum | solution.py:97
  10.6 2.0 copy-start.7
  13.6 2.0 copy-start.8
  16.8 1.5 copy-start.15
  16.8 1.9 copy-start.14
  16.8 2.0 copy-start.16
  16.8 39.0 %copy-start.11 = (bf16[64,8,4,256]{3,1,2,0:T(8,128)(2,1)S(1)}, bf16[64,8,4,256]{3,1,2,0:T(8,128)(2,1)}, u32[]{:S(2)}) copy-start(bf16[64,8,4,256]{3,1,2,0:T(8,128)(2,1)} %copy.22) | copy-start | bytes 3145732
  52.5 3.3 copy-start
  58.4 1.3 copy-start.6
  77.0 2.3 copy-start.9
  77.0 2.3 copy-start.10
  79.2 126.9 %all-gather.8.cloned.1.call-start = ((), (), s32[]{:S(2)}) async-start(), calls=%async_computation.3 | async-start | bytes 3145728 | tf_op jit(solution)/shard_map/all_gather | solution.py:119
  191.9 4.5 %copy-start.1 = (bf16[1,512,4,256]{3,2,1,0:T(4,128)(2,1)S(1)}, bf16[1,512,4,256]{3,2,1,0:T(4,128)(2,1)}, u32[]{:S(2)}) copy-start(bf16[1,512,4,256]{3,2,1,0:T(4,128)(2,1)} %get-tuple-element.422) | copy-start | bytes 3145732
  193.6 4.0 %copy-start.2 = (bf16[1,2048,256]{2,1,0:T(8,128)(2,1)S(1)}, bf16[1,2048,256]{2,1,0:T(8,128)(2,1)}, u32[]{:S(2)}) copy-start(bf16[1,2048,256]{2,1,0:T(8,128)(2,1)} %get-tuple-element.426) | copy-start | bytes 3145732
  196.2 141.1 %all-reduce.7.cloned.1.call-start = ((), (), s32[]{:S(2)}) async-start(), calls=%async_computation.2 | async-start | bytes 1048576 | tf_op jit(solution)/shard_map/psum | solution.py:97
  197.6 1.4 copy-start.3
  209.0 1.8 copy-start.12
  213.5 1.7 copy-start.4
  229.4 107.9 %copy-start.5 = (bf16[1024,1024]{0,1:T(8,128)(2,1)S(1)}, bf16[1024,1024]{0,1:T(8,128)(2,1)}, u32[]{:S(2)}) copy-start(bf16[1024,1024]{0,1:T(8,128)(2,1)} %copy-done.4) | copy-start | bytes 6291460
  230.3 123.5 %all-gather.10.cloned.1.call-start = ((), (), s32[]{:S(2)}) async-start(), calls=%async_computation.4 | async-start | bytes 3145728 | tf_op jit(solution)/shard_map/all_gather | solution.py:119
  230.3 112.1 %copy-start.13 = (bf16[2,256,512]{2,1,0:T(8,128)(2,1)S(1)}, bf16[2,256,512]{2,1,0:T(8,128)(2,1)}, u32[]{:S(2)}) copy-start(bf16[2,256,512]{2,1,0:T(8,128)(2,1)} %param.27) | copy-start | bytes 1572868
Sparse Core Ops, SparseCore 0:
  9.5 42.9 all-gather.5
  79.3 108.5 all-reduce.4
  196.3 9.7 all-gather.7
  230.4 106.7 all-reduce.6
  344.0 9.7 all-gather.9
